TPU v7x, 256 devices: a whole 4x4x8 slice. The times are simulated.
256 devices in a mesh: xy: 32 (over z, x_lo, core), gz: 8 (over y, x_hi).
Axes of the slice: x: 4 (x_hi: 2, x_lo: 2; x = x_hi * 2 + x_lo), y: 4, z: 8, core: 2. Of those that a mesh axis runs over, the one named last changes fastest.
Arguments:
- file_data: float32 [512, 64, 8192], P('gz', None, 'xy')
- factor: float32 [512, 256], P('gz'), may hold values from -0.25 to 0.25
- block_owner: int32 [64], replicated, may hold values from 0 to 31, as said below
- block_offset: int32 [64], replicated, may hold values from 0 to 128, as said below
Outputs:
- gram: float32 [512, 512], P('gz')
- core: float32 [256, 64, 8192], P('gz', None, 'xy')
Inputs may be any that keep to these rules, and one draw needn't show every extreme that they name: `block_owner`: block b of device d (b = d * 2 + j) is owned by d - 1, d or d + 1 modulo 32. Every index of xy owns exactly 2 blocks. `block_offset`: offsets are multiples of 128; the blocks of one owner take distinct offsets, so every file slot is named once.
All inputs are finite; a program needn't handle non-finite values.
Results may differ from a plain program's by a relative error of at most 0.00007.
Values sent between devices are 32-bit elements; how exact they have to be, the bound alone decides.
A program may use at most 128 MiB of HBM per device.

v0:
```python
import jax
import jax.numpy as jnp
from jax import lax
from jax.sharding import PartitionSpec as P

BLOCKS_DEV = 2


def shifted(array, axis, by):
    length = lax.axis_size(axis)
    return lax.ppermute(array, axis, [(i, (i + by) % length) for i in range(length)])


def split_up(array, dim, length):
    shape = array.shape
    tiles = array.reshape(*shape[:dim], length, shape[dim] // length, *shape[dim + 1 :])
    return jnp.moveaxis(tiles, dim, 0)


def sent_and_summed(array, axis, dim):
    length = lax.axis_size(axis)
    tiles = lax.all_to_all(split_up(array, dim, length), axis, 0, 0, tiled=True)
    return jnp.sum(tiles, axis=0)


def over_pieces(array, axis):
    tiles = lax.all_gather(array, axis)
    return tiles.sum(axis=0)


def sent_to_all(array, axis):
    length = lax.axis_size(axis)
    return lax.all_to_all(
        jnp.broadcast_to(array[None], (length, *array.shape)), axis, 0, 0, tiled=True
    )


def joined_along(tiles, dim):
    tiles = jnp.moveaxis(tiles, 0, dim)
    shape = tiles.shape
    return tiles.reshape(*shape[:dim], shape[dim] * shape[dim + 1], *shape[dim + 2 :])


def gather_directly(array, axis, dim):
    tiles = sent_to_all(array, axis)
    return joined_along(tiles, dim)


def take_block(buffer, offset):
    return lax.dynamic_slice_in_dim(buffer, offset, 128, 2)


def rebalance(buffer, block_owner, block_offset):
    devices = lax.axis_size("xy")
    myself = lax.axis_index("xy")
    lower_peer = (myself + devices - 1) % devices
    upper_peer = (myself + 1) % devices
    blank = jnp.zeros(buffer.shape[:2] + (128,), buffer.dtype)

    def outgoing(target):
        pieces = []
        for j in range(BLOCKS_DEV):
            owner = block_owner[target * BLOCKS_DEV + j]
            offset = block_offset[target * BLOCKS_DEV + j]
            pieces.append(jnp.where(owner == myself, take_block(buffer, offset), blank))
        return jnp.concatenate(pieces, axis=2)

    from_lower = shifted(outgoing(upper_peer), "xy", 1)
    from_upper = shifted(outgoing(lower_peer), "xy", -1)
    blocks = []
    for j in range(BLOCKS_DEV):
        owner = block_owner[myself * BLOCKS_DEV + j]
        offset = block_offset[myself * BLOCKS_DEV + j]
        local_block = take_block(buffer, offset)
        lower_block = from_lower[:, :, j * 128 : (j + 1) * 128]
        upper_block = from_upper[:, :, j * 128 : (j + 1) * 128]
        remote = jnp.where(owner == lower_peer, lower_block, upper_block)
        blocks.append(jnp.where(owner == myself, local_block, remote))
    return jnp.concatenate(blocks, axis=2)


def used_slots(file_data, block_owner, block_offset):
    myself = lax.axis_index("xy")
    slot_count = file_data.shape[2] // 128
    hits = (block_owner[:, None] == myself) & (
        block_offset[:, None] // 128 == jnp.arange(slot_count, dtype=jnp.int32)[None, :]
    )
    used = jnp.any(hits, axis=0).astype(jnp.float32)
    return jnp.repeat(used, 128)


def local(file_data, factor, block_owner, block_offset):
    working = file_data * used_slots(file_data, block_owner, block_offset)[None, None, :]
    swapped = lax.all_to_all(working, "gz", split_axis=1, concat_axis=0, tiled=True)
    scale = 1.0 / (BLOCKS_DEV * 128 * lax.axis_size("xy") * file_data.shape[1])
    partial_gram = (
        jnp.einsum("zcs,wcs->zw", swapped, swapped, precision=lax.Precision.HIGHEST) * scale
    )
    gram_block = sent_and_summed(partial_gram, "gz", 0)
    gram = over_pieces(gram_block, "xy")
    whole_factor = gather_directly(factor, "gz", 0)
    core_part = jnp.einsum("zr,zcs->rcs", whole_factor, swapped, precision=lax.Precision.HIGHEST)
    core = lax.all_to_all(core_part, "gz", split_axis=0, concat_axis=1, tiled=True)
    core = rebalance(core, block_owner, block_offset)
    return (gram, core)


def solution(mesh):
    return jax.shard_map(
        local,
        mesh=mesh,
        in_specs=(P("gz", None, "xy"), P("gz", None), P(), P()),
        out_specs=(P("gz", None), P("gz", None, "xy")),
        check_vma=False,
    )
```

profile of v0, /device:TPU:1, one launch (start us, length us, event | category | flops | bytes accessed | tf_op | source)
XLA Modules:
  0.0 235.7 jit_solution(13166197315982324203)
XLA Ops:
  7.2 0.7 and_select_fusion
  7.9 0.7 broadcast_compare_fusion
  8.7 4.6 %copy_multiply_fusion = f32[64,64,256]{2,0,1:T(8,128)S(1)} fusion(f32[64,64,256]{2,1,0:T(8,128)} %param.4, f32[256]{0:T(256)S(1)} %broadcast_bitcast_fusion), kind=kLoop, calls=%fused_computation.2 | loop fusion | flops 1048576 | bytes 8389632 | tf_op jit(solution)/shard_map/mul | solution.py:93
  13.4 57.3 %all_to_all.46 = f32[64,64,256]{2,0,1:T(8,128)S(1)} all-to-all(f32[64,64,256]{2,0,1:T(8,128)S(1)} %copy_multiply_fusion), channel_id=1, replica_groups=mesh['xy'=32,'gz'=8] {'gz'}, dimensions={1} | all-to-all | bytes 8388608 | tf_op jit(solution)/shard_map/all_to_all | solution.py:94
  71.2 1.5 copy-done
  72.7 6.9 %fusion.5 = f32[512,512]{1,0:T(8,128)S(1)} fusion(f32[512,8,256]{2,0,1:T(8,128)S(1)} %bitcast.44), kind=kOutput, calls=%fused_computation.9 | convolution fusion | flops 6442713088 | bytes 5242880 | tf_op jit(solution)/shard_map/zcs,wcs->zw/dot_general | solution.py:97
  79.6 18.5 %all_to_all.47 = f32[8,64,512]{2,1,0:T(8,128)S(1)} all-to-all(f32[8,64,512]{2,1,0:T(8,128)S(1)} %bitcast.50), channel_id=1, replica_groups=mesh['xy'=32,'gz'=8] {'gz'}, dimensions={0} | all-to-all | bytes 2097152 | tf_op jit(solution)/shard_map/all_to_all | solution.py:22
  98.1 0.7 reduce_sum.18
  98.9 11.5 %all_to_all.48 = f32[8,64,256]{2,1,0:T(8,128)S(1)} all-to-all(f32[8,64,256]{2,1,0:T(8,128)S(1)} %broadcast_in_dim.7), channel_id=1, replica_groups=mesh['xy'=32,'gz'=8] {'gz'}, dimensions={0} | all-to-all | bytes 1048576 | tf_op jit(solution)/shard_map/all_to_all | solution.py:33
  110.3 8.6 %fusion.2 = f32[256,8,256]{0,2,1:T(8,128)S(1)} fusion(f32[8,64,256]{2,1,0:T(8,128)S(1)} %all_to_all.48, f32[64,8,8,256]{3,0,2,1:T(8,128)} %bitcast.48), kind=kOutput, calls=%fused_computation.7 | convolution fusion | flops 3221225472 | bytes 6815744 | tf_op jit(solution)/shard_map/zr,zcs->rcs/dot_general | solution.py:102
  118.9 2.0 copy.20
  120.9 3.7 %all-to-all-start.3 = ((f32[256,8,256]{2,1,0:T(8,128)}), f32[256,8,256]{2,1,0:T(8,128)S(1)}, u32[]{:S(2)}, u32[]{:S(2)}) async-start(f32[256,8,256]{2,1,0:T(8,128)} %copy.20), calls=%async_computation.3 | async-start | bytes 4194304 | tf_op jit(solution)/shard_map/all_to_all | solution.py:103
  124.7 0.7 fusion.10
  135.7 29.0 %all-to-all-done.3 = f32[256,8,256]{2,1,0:T(8,128)S(1)} async-done(((f32[256,8,256]{2,1,0:T(8,128)}), f32[256,8,256]{2,1,0:T(8,128)S(1)}, u32[]{:S(2)}, u32[]{:S(2)}) %all-to-all-start.3) | async-done | bytes 2097184 | tf_op jit(solution)/shard_map/all_to_all | solution.py:103
  164.7 1.3 copy-done.1
  166.0 1.9 copy.31
  167.9 1.2 dynamic-slice_select_fusion.3
  169.1 1.5 pad_maximum_fusion.1
  170.5 3.9 %collective-permute-start.1 = (f32[32,64,256]{2,1,0:T(8,128)}, f32[32,64,256]{2,1,0:T(8,128)}, u32[]{:S(2)}, u32[]{:S(2)}) collective-permute-start(f32[32,64,256]{2,1,0:T(8,128)} %pad_maximum_fusion.1), channel_id=1, source_target_pairs={{0,248},{8,0},{16,8},{24,16},{32,24},{40,32},{48,40},{56,48},{64,5... | collective-permute-start | bytes 6291464 | tf_op jit(solution)/shard_map/ppermute | solution.py:11
  174.5 1.5 pad_maximum_fusion
  182.3 38.9 %collective-permute-done.1 = f32[32,64,256]{2,1,0:T(8,128)} collective-permute-done((f32[32,64,256]{2,1,0:T(8,128)}, f32[32,64,256]{2,1,0:T(8,128)}, u32[]{:S(2)}, u32[]{:S(2)}) %collective-permute-start.1) | collective-permute-done | bytes 2097184 | tf_op jit(solution)/shard_map/ppermute | solution.py:11
  221.3 2.9 %fusion.7 = (f32[32,64,128]{2,1,0:T(8,128)S(1)}, f32[32,64,128]{2,1,0:T(8,128)S(1)}) fusion(f32[32,64,256]{2,1,0:T(8,128)} %collective-permute-done.1, f32[32,64,256]{2,1,0:T(8,128)} %collective-permute-done, f32[32,64,256]{2,1,0:T(8,128)S(1)} %bitcast.46, s32[]{:T(128)S(6)} %select_n.112, pred[]{:T(512)S(6)} %eq.53, pred[]{:T(512)S(6)} %eq.52, pred[]{:T(512)S(6)} %eq.59, ...), kind=kLoop, calls=%fused_computation.13 | loop fusion | flops 1048576 | bytes 8388620 | tf_op jit(solution)/shard_map/jit(_where)/select_n | solution.py:78
  224.2 1.5 pad_maximum_fusion.2
  225.7 3.2 %reduce_sum.19 = f32[64,512]{1,0:T(8,128)} reduce(f32[32,64,512]{2,1,0:T(8,128)} %bitcast.51, f32[]{:T(128)} %constant.52.clone.1), dimensions={0}, to_apply=%region_2.3 | reduce | flops 1015808 | bytes 4325380 | tf_op jit(solution)/shard_map/reduce_sum | solution.py:28
  (18 shorter events, 1.1 us)
Async XLA Ops:
  7.2 218.5 %all-gather.3.cloned.1.call-start = ((), (), s32[]{:S(2)}) async-start(), calls=%async_computation.4 | async-start | bytes 4325376 | tf_op jit(solution)/shard_map/all_gather | solution.py:27
  70.7 2.0 copy-start
  79.6 19.2 %copy-start.2 = (f32[64,256]{1,0:T(8,128)S(1)}, f32[64,256]{1,0:T(8,128)}, u32[]{:S(2)}) copy-start(f32[64,256]{1,0:T(8,128)} %param.5) | copy-start | bytes 196612
  120.9 3.8 %copy-start.3 = (s32[64]{0:T(128)S(1)}, s32[64]{0:T(128)}, u32[]{:S(2)}) copy-start(s32[64]{0:T(128)} %param.6) | copy-start | bytes 772
  120.9 3.8 %copy-start.4 = (s32[64]{0:T(128)S(1)}, s32[64]{0:T(128)}, u32[]{:S(2)}) copy-start(s32[64]{0:T(128)} %param.7) | copy-start | bytes 772
  120.9 43.8 %all-to-all-start.3 = ((f32[256,8,256]{2,1,0:T(8,128)}), f32[256,8,256]{2,1,0:T(8,128)S(1)}, u32[]{:S(2)}, u32[]{:S(2)}) async-start(f32[256,8,256]{2,1,0:T(8,128)} %copy.20), calls=%async_computation.3 | async-start | bytes 4194304 | tf_op jit(solution)/shard_map/all_to_all | solution.py:103
  164.7 1.3 copy-start.1
  170.5 50.7 %collective-permute-start.1 = (f32[32,64,256]{2,1,0:T(8,128)}, f32[32,64,256]{2,1,0:T(8,128)}, u32[]{:S(2)}, u32[]{:S(2)}) collective-permute-start(f32[32,64,256]{2,1,0:T(8,128)} %pad_maximum_fusion.1), channel_id=1, source_target_pairs={{0,248},{8,0},{16,8},{24,16},{32,24},{40,32},{48,40},{56,48},{64,5... | collective-permute-start | bytes 6291464 | tf_op jit(solution)/shard_map/ppermute | solution.py:11
  176.0 45.3 %collective-permute-start = (f32[32,64,256]{2,1,0:T(8,128)}, f32[32,64,256]{2,1,0:T(8,128)}, u32[]{:S(2)}, u32[]{:S(2)}) collective-permute-start(f32[32,64,256]{2,1,0:T(8,128)} %pad_maximum_fusion), channel_id=1, source_target_pairs={{0,8},{8,16},{16,24},{24,32},{32,40},{40,48},{48,56},{56,64},{64,7... | collective-permute-start | bytes 6291464 | tf_op jit(solution)/shard_map/ppermute | solution.py:11
Sparse Core Ops, SparseCore 0:
  98.9 67.6 all-gather.2
where the time goes:
time: 236 us
  blocking collectives  87.3 us (37%)
  waiting for transfers between devices  68 us (29%)
  between operations  30.5 us (13%)
  other arithmetic  18.6 us (8%)
  matrix products  15.5 us (7%)
  starting transfers between devices  8 us (3%)
  local copies, waits for them, and re-layouts  7.97 us (3%)
    all_to_all x1, blocking collectives, local(): lax.all_to_all(working, 'gz', split_axis=1, concat_axis=0, tiled=True)  57.3 us
    ppermute x2, waiting for transfers between devices, shifted(): lax.ppermute(array, axis, [(i, (i + by) % length) for i in range(length)])  38.9 us
    all_to_all x1, waiting for transfers between devices, local(): lax.all_to_all(core_part, 'gz', split_axis=0, concat_axis=1, tiled=True)  29 us
    all_to_all x1, blocking collectives, sent_and_summed(): tiles = lax.all_to_all(split_up(array, dim, length), axis, 0, 0, tiled=True)  18.5 us
    all_to_all x1, blocking collectives, sent_to_all(): lax.all_to_all(jnp.broadcast_to(array[None], (length, *array.shape)), axi...  11.5 us
    dot_general x1, matrix products, local(): jnp.einsum('zr,zcs->rcs', whole_factor, swapped, precision=lax.Precision....  8.57 us
    dot_general x1, matrix products, local(): jnp.einsum('zcs,wcs->zw', swapped, swapped, precision=lax.Precision.HIGHEST)  6.89 us
  transfers between devices with their start and end apart: 4, of which 2 were waited for; matrix products, arithmetic and copies ran while one was open for 9% of the time, Pallas kernels for 0%

commit v1 on v0

--- a/solution.py
+++ b/solution.py
@@ -91,7 +91,10 @@
 
 def local(file_data, factor, block_owner, block_offset):
     working = file_data * used_slots(file_data, block_owner, block_offset)[None, None, :]
-    swapped = lax.all_to_all(working, "gz", split_axis=1, concat_axis=0, tiled=True)
+    swapped = jnp.concatenate(
+        lax.all_to_all(jnp.stack(jnp.split(working, lax.axis_size("gz"), axis=1)), "gz", 0, 0),
+        axis=0,
+    )
     scale = 1.0 / (BLOCKS_DEV * 128 * lax.axis_size("xy") * file_data.shape[1])
     partial_gram = (
         jnp.einsum("zcs,wcs->zw", swapped, swapped, precision=lax.Precision.HIGHEST) * scale

time: 236 us -> 236 us (level)
  no operation moved by 1% of the time
where the time goes in v1:
time: 236 us
  blocking collectives  87.1 us (37%)
  waiting for transfers between devices  67.9 us (29%)
  between operations  30.6 us (13%)
  other arithmetic  18.6 us (8%)
  matrix products  15.5 us (7%)
  local copies, waits for them, and re-layouts  8.26 us (4%)
  starting transfers between devices  7.86 us (3%)
    all_to_all x1, blocking collectives, local(): lax.all_to_all(jnp.stack(jnp.split(working, lax.axis_size('gz'), axis=1))...  57.3 us
    ppermute x2, waiting for transfers between devices, shifted(): lax.ppermute(array, axis, [(i, (i + by) % length) for i in range(length)])  38.9 us
    all_to_all x1, waiting for transfers between devices, local(): lax.all_to_all(core_part, 'gz', split_axis=0, concat_axis=1, tiled=True)  29 us
    all_to_all x1, blocking collectives, sent_and_summed(): tiles = lax.all_to_all(split_up(array, dim, length), axis, 0, 0, tiled=True)  18.4 us
    all_to_all x1, blocking collectives, sent_to_all(): lax.all_to_all(jnp.broadcast_to(array[None], (length, *array.shape)), axi...  11.5 us
    dot_general x1, matrix products, local(): jnp.einsum('zr,zcs->rcs', whole_factor, swapped, precision=lax.Precision....  8.57 us
    dot_general x1, matrix products, local(): jnp.einsum('zcs,wcs->zw', swapped, swapped, precision=lax.Precision.HIGHEST)  6.89 us
  transfers between devices with their start and end apart: 4, of which 2 were waited for; matrix products, arithmetic and copies ran while one was open for 9% of the time, Pallas kernels for 0%

profile of v1, /device:TPU:1, one launch (start us, length us, event | category | flops | bytes accessed | tf_op | source)
XLA Modules:
  0.0 235.8 jit_solution(8690321319621518419)
XLA Ops:
  7.2 0.7 and_select_fusion
  7.9 0.7 broadcast_compare_fusion
  8.7 4.6 %copy_multiply_fusion = f32[64,64,256]{2,0,1:T(8,128)S(1)} fusion(f32[64,64,256]{2,1,0:T(8,128)} %param.4, f32[256]{0:T(256)S(1)} %broadcast_bitcast_fusion), kind=kLoop, calls=%fused_computation | loop fusion | flops 1048576 | bytes 8389632 | tf_op jit(solution)/shard_map/mul | solution.py:93
  13.7 57.3 %all_to_all.33 = f32[8,64,8,256]{3,1,2,0:T(8,128)S(1)} all-to-all(f32[8,64,8,256]{3,1,2,0:T(8,128)S(1)} %fusion.3), channel_id=1, replica_groups=mesh['xy'=32,'gz'=8] {'gz'}, dimensions={0} | all-to-all | bytes 8388608 | tf_op jit(solution)/shard_map/all_to_all | solution.py:95
  71.5 1.5 copy-done
  73.0 6.9 %fusion = f32[512,512]{1,0:T(8,128)S(1)} fusion(f32[512,8,256]{2,0,1:T(8,128)S(1)} %bitcast.71), kind=kOutput, calls=%fused_computation.7 | convolution fusion | flops 6442713088 | bytes 5242880 | tf_op jit(solution)/shard_map/zcs,wcs->zw/dot_general | solution.py:100
  79.9 18.4 %all_to_all.34 = f32[8,64,512]{2,1,0:T(8,128)S(1)} all-to-all(f32[8,64,512]{2,1,0:T(8,128)S(1)} %bitcast.75), channel_id=1, replica_groups=mesh['xy'=32,'gz'=8] {'gz'}, dimensions={0} | all-to-all | bytes 2097152 | tf_op jit(solution)/shard_map/all_to_all | solution.py:22
  98.3 0.7 reduce_sum.18
  99.1 11.5 %all_to_all.35 = f32[8,64,256]{2,1,0:T(8,128)S(1)} all-to-all(f32[8,64,256]{2,1,0:T(8,128)S(1)} %broadcast_in_dim.7), channel_id=1, replica_groups=mesh['xy'=32,'gz'=8] {'gz'}, dimensions={0} | all-to-all | bytes 1048576 | tf_op jit(solution)/shard_map/all_to_all | solution.py:33
  110.6 8.6 %convolution_bitcast_fusion = f32[256,8,256]{0,2,1:T(8,128)S(1)} fusion(f32[8,64,8,256]{3,1,2,0:T(8,128)} %copy-done, f32[8,64,256]{2,1,0:T(8,128)S(1)} %all_to_all.35), kind=kOutput, calls=%fused_computation.5 | convolution fusion | flops 3221225472 | bytes 6815744 | tf_op jit(solution)/shard_map/zr,zcs->rcs/dot_general | solution.py:105
  119.2 2.0 copy.41
  121.1 3.6 %all-to-all-start.3 = ((f32[256,8,256]{2,1,0:T(8,128)}), f32[256,8,256]{2,1,0:T(8,128)S(1)}, u32[]{:S(2)}, u32[]{:S(2)}) async-start(f32[256,8,256]{2,1,0:T(8,128)} %copy.41), calls=%async_computation.3 | async-start | bytes 4194304 | tf_op jit(solution)/shard_map/all_to_all | solution.py:106
  124.8 0.7 fusion.12
  135.8 29.0 %all-to-all-done.3 = f32[256,8,256]{2,1,0:T(8,128)S(1)} async-done(((f32[256,8,256]{2,1,0:T(8,128)}), f32[256,8,256]{2,1,0:T(8,128)S(1)}, u32[]{:S(2)}, u32[]{:S(2)}) %all-to-all-start.3) | async-done | bytes 2097184 | tf_op jit(solution)/shard_map/all_to_all | solution.py:106
  164.8 1.3 copy-done.1
  166.1 1.9 copy.46
  167.9 1.2 dynamic-slice_select_fusion.3
  169.1 1.5 pad_maximum_fusion.1
  170.6 3.9 %collective-permute-start.1 = (f32[32,64,256]{2,1,0:T(8,128)}, f32[32,64,256]{2,1,0:T(8,128)}, u32[]{:S(2)}, u32[]{:S(2)}) collective-permute-start(f32[32,64,256]{2,1,0:T(8,128)} %pad_maximum_fusion.1), channel_id=1, source_target_pairs={{0,248},{8,0},{16,8},{24,16},{32,24},{40,32},{48,40},{56,48},{64,5... | collective-permute-start | bytes 6291464 | tf_op jit(solution)/shard_map/ppermute | solution.py:11
  174.5 1.5 pad_maximum_fusion
  182.4 38.9 %collective-permute-done.1 = f32[32,64,256]{2,1,0:T(8,128)} collective-permute-done((f32[32,64,256]{2,1,0:T(8,128)}, f32[32,64,256]{2,1,0:T(8,128)}, u32[]{:S(2)}, u32[]{:S(2)}) %collective-permute-start.1) | collective-permute-done | bytes 2097184 | tf_op jit(solution)/shard_map/ppermute | solution.py:11
  221.3 2.9 %fusion.2 = (f32[32,64,128]{2,1,0:T(8,128)S(1)}, f32[32,64,128]{2,1,0:T(8,128)S(1)}) fusion(f32[32,64,256]{2,1,0:T(8,128)} %collective-permute-done.1, f32[32,64,256]{2,1,0:T(8,128)} %collective-permute-done, f32[32,64,256]{2,1,0:T(8,128)S(1)} %bitcast.73, s32[]{:T(128)S(6)} %select_n.112, pred[]{:T(512)S(6)} %eq.53, pred[]{:T(512)S(6)} %eq.52, pred[]{:T(512)S(6)} %eq.59, ...), kind=kLoop, calls=%fused_computation.11 | loop fusion | flops 1048576 | bytes 8388620 | tf_op jit(solution)/shard_map/jit(_where)/select_n | solution.py:78
  224.2 1.5 pad_maximum_fusion.2
  225.7 3.2 %reduce_sum.19 = f32[64,512]{1,0:T(8,128)} reduce(f32[32,64,512]{2,1,0:T(8,128)} %bitcast.76, f32[]{:T(128)} %constant.52.clone.1), dimensions={0}, to_apply=%region_2.3 | reduce | flops 1015808 | bytes 4325380 | tf_op jit(solution)/shard_map/reduce_sum | solution.py:28
  (26 shorter events, 1.4 us)
Async XLA Ops:
  7.2 218.6 %all-gather.3.cloned.1.call-start = ((), (), s32[]{:S(2)}) async-start(), calls=%async_computation.4 | async-start | bytes 4325376 | tf_op jit(solution)/shard_map/all_gather | solution.py:27
  71.0 2.0 copy-start
  73.0 26.0 %copy-start.2 = (f32[64,256]{1,0:T(8,128)S(1)}, f32[64,256]{1,0:T(8,128)}, u32[]{:S(2)}) copy-start(f32[64,256]{1,0:T(8,128)} %param.5) | copy-start | bytes 196612
  119.1 5.7 %copy-start.3 = (s32[64]{0:T(128)S(1)}, s32[64]{0:T(128)}, u32[]{:S(2)}) copy-start(s32[64]{0:T(128)} %param.6) | copy-start | bytes 772
  119.2 5.6 %copy-start.4 = (s32[64]{0:T(128)S(1)}, s32[64]{0:T(128)}, u32[]{:S(2)}) copy-start(s32[64]{0:T(128)} %param.7) | copy-start | bytes 772
  121.1 43.6 %all-to-all-start.3 = ((f32[256,8,256]{2,1,0:T(8,128)}), f32[256,8,256]{2,1,0:T(8,128)S(1)}, u32[]{:S(2)}, u32[]{:S(2)}) async-start(f32[256,8,256]{2,1,0:T(8,128)} %copy.41), calls=%async_computation.3 | async-start | bytes 4194304 | tf_op jit(solution)/shard_map/all_to_all | solution.py:106
  164.8 1.3 copy-start.1
  170.6 50.7 %collective-permute-start.1 = (f32[32,64,256]{2,1,0:T(8,128)}, f32[32,64,256]{2,1,0:T(8,128)}, u32[]{:S(2)}, u32[]{:S(2)}) collective-permute-start(f32[32,64,256]{2,1,0:T(8,128)} %pad_maximum_fusion.1), channel_id=1, source_target_pairs={{0,248},{8,0},{16,8},{24,16},{32,24},{40,32},{48,40},{56,48},{64,5... | collective-permute-start | bytes 6291464 | tf_op jit(solution)/shard_map/ppermute | solution.py:11
  176.0 45.3 %collective-permute-start = (f32[32,64,256]{2,1,0:T(8,128)}, f32[32,64,256]{2,1,0:T(8,128)}, u32[]{:S(2)}, u32[]{:S(2)}) collective-permute-start(f32[32,64,256]{2,1,0:T(8,128)} %pad_maximum_fusion), channel_id=1, source_target_pairs={{0,8},{8,16},{16,24},{24,32},{32,40},{40,48},{48,56},{56,64},{64,7... | collective-permute-start | bytes 6291464 | tf_op jit(solution)/shard_map/ppermute | solution.py:11
Sparse Core Ops, SparseCore 0:
  99.2 67.4 all-gather.2
